TPU v7x, 32 devices: a whole 2x2x4 slice. The times are simulated.
32 devices in a mesh: ctx: 16 (over z, y, core), head: 2 (over x).
Axes of the slice: x: 2, y: 2, z: 4, core: 2. Of those that a mesh axis runs over, the one named last changes fastest.
Arguments:
- queries: bfloat16 [2048, 8192], P('ctx', 'head'), may hold values from -5.5 to 5.5
- keys: bfloat16 [2048, 1024], P('ctx', 'head'), may hold values from -5.5 to 5.5
- values: bfloat16 [2048, 1024], P('ctx', 'head'), may hold values from -6 to 6
- feature_weights: bfloat16 [64, 128, 64], P('head'), may hold values from -1 to 1
Outputs:
- attn_error: float32 [2048, 8192], P('ctx', 'head')
- loss: float32 [], replicated
- grad_w: float32 [64, 128, 64], P('head')
All inputs are finite; a program needn't handle non-finite values.
Results may differ from a plain program's by a relative error of at most 0.004.
Values may be sent and summed in bfloat16 or wider, within the bound.
No kernel may reach another device: no remote copies, remote signals or barrier semaphores. Data moves between devices by JAX's collectives and lax.ppermute only.
A program may use at most 192 MiB of HBM per device.

v0:
```python
import math
import jax
import jax.numpy as jnp
from jax import lax
from jax.sharding import PartitionSpec as P

HEAD_SIZE = 128
QUERY_HEADS = 64
KEY_VALUE_HEADS = 8
FM = 64
WIN = 64
phi_scale = 0.00390625
big_negative = -1e30
highest = lax.Precision.HIGHEST


def swapped(value, axis, distance):
    mask = 2**distance
    pairs = [(source, source ^ mask) for source in range(lax.axis_size(axis))]
    return lax.ppermute(value, axis, pairs)


def carried_in(value, axis, combine, identity):
    devices, here = (lax.axis_size(axis), lax.axis_index(axis))
    everything = jax.tree.map(
        lambda part, kind: lax.all_gather(part.astype(kind), axis),
        value,
        (jnp.bfloat16, jnp.bfloat16),
    )
    start = jax.tree.map(
        lambda part, zero: jnp.broadcast_to(jnp.asarray(zero, part.dtype), part.shape),
        value,
        identity,
    )

    def carried_step(k, before):
        reached = k < here
        new = combine(
            before, jax.tree.map(lambda part, own: part[k].astype(own.dtype), everything, value)
        )
        return jax.tree.map(lambda a, b: jnp.where(reached, a, b), new, before)

    return lax.fori_loop(0, devices, carried_step, start)


def prefix(value, axis, combine, identity):
    devices, here = (lax.axis_size(axis), lax.axis_index(axis))
    everything = jax.tree.map(
        lambda part, kind: lax.all_gather(part.astype(kind), axis),
        value,
        jax.tree.map(lambda a: jnp.bfloat16 if a.dtype == jnp.float32 else a.dtype, value),
    )
    start = jax.tree.map(
        lambda part, zero: jnp.broadcast_to(jnp.asarray(zero, part.dtype), part.shape),
        value,
        identity,
    )

    def prefix_step(k, before):
        at = devices - 1 - k
        reached = at > here
        new = combine(
            before, jax.tree.map(lambda part, own: part[at].astype(own.dtype), everything, value)
        )
        return jax.tree.map(lambda a, b: jnp.where(reached, a, b), new, before)

    return lax.fori_loop(0, devices, prefix_step, start)


def features(projection):
    return phi_scale * jnp.concatenate(
        [1.0 + jax.nn.elu(projection), 1.0 + jax.nn.elu(-projection)], axis=-1
    )


def feature_back(projection, grad_phi):
    half = projection.shape[-1]
    slope_plus = jnp.where(projection > 0, 1.0, jnp.exp(jnp.minimum(projection, 0.0)))
    slope_minus = jnp.where(projection < 0, 1.0, jnp.exp(jnp.minimum(-projection, 0.0)))
    return phi_scale * (grad_phi[..., :half] * slope_plus - grad_phi[..., half:] * slope_minus)


def add_pair(earlier, later):
    return (earlier[0] + later[0], earlier[1] + later[1])


def split_product(form, phi_part, data):
    upper = phi_part.astype(jnp.bfloat16)
    lower = (phi_part - upper.astype(jnp.float32)).astype(jnp.bfloat16)
    return jnp.einsum(form, upper, data, preferred_element_type=jnp.float32) + jnp.einsum(
        form, lower, data, preferred_element_type=jnp.float32
    )


def visit_partner(rows):
    for bit_index in range(lax.axis_size("ctx").bit_length() - 1):
        rows = swapped(rows, "ctx", bit_index)
    return rows


def return_partner(rows):
    for bit_index in range(lax.axis_size("ctx").bit_length() - 1):
        rows = swapped(rows.astype(jnp.bfloat16), "ctx", bit_index).astype(rows.dtype)
    return rows


def teacher_part(part, query_set, pos_set, key_block, value_block, key_pos, masked):
    scale_factor = 1.0 / math.sqrt(query_set.shape[-1])
    scores = (
        jnp.einsum("qgrd,kgd->grqk", query_set, key_block, preferred_element_type=jnp.float32)
        * scale_factor
    )
    if masked:
        causal = key_pos[None, :] <= pos_set[:, None]
        top = jnp.maximum(part[0], jnp.max(jnp.where(causal, scores, big_negative), axis=-1))
        weights = jnp.exp(jnp.where(causal, scores - top[..., None], big_negative))
    else:
        top = jnp.maximum(part[0], jnp.max(scores, axis=-1))
        weights = jnp.exp(scores - top[..., None])
    rescale = jnp.exp(part[0] - top)
    total = part[1] * rescale + jnp.sum(weights, axis=-1)
    mixed = part[2] * rescale[..., None] + jnp.einsum(
        "grqk,kgd->grqd",
        weights.astype(jnp.bfloat16),
        value_block,
        preferred_element_type=jnp.float32,
    )
    return (top, total, mixed)


def advance(part, row_set, key_block, value_block, key_pos, first):
    query_set, pos_set = row_set
    needed = first <= pos_set[-1]
    straddle = key_pos[-1] > pos_set[0]
    branch_index = jnp.where(needed, jnp.where(straddle, 2, 1), 0).astype(jnp.int32)
    return lax.switch(
        branch_index,
        [
            lambda current: current,
            lambda current: teacher_part(
                current, query_set, pos_set, key_block, value_block, key_pos, False
            ),
            lambda current: teacher_part(
                current, query_set, pos_set, key_block, value_block, key_pos, True
            ),
        ],
        part,
    )


def shards(queries, keys, values, feature_weights):
    local_rows = queries.shape[0]
    half_rows = local_rows // 2
    groups = keys.shape[1] // HEAD_SIZE
    group_ratio = QUERY_HEADS // KEY_VALUE_HEADS
    heads_here = groups * group_ratio
    ctx_count = lax.axis_size("ctx")
    ctx_place = lax.axis_index("ctx")
    own_start = ctx_place * local_rows
    query4 = queries.reshape(local_rows, groups, group_ratio, HEAD_SIZE)
    own_keys = keys.reshape(local_rows, groups, HEAD_SIZE)
    own_values = values.reshape(local_rows, groups, HEAD_SIZE)
    weight4 = feature_weights.reshape(groups, group_ratio, HEAD_SIZE, FM)
    scale = 1.0 / math.sqrt(HEAD_SIZE)
    query_pos = own_start + jnp.arange(local_rows, dtype=jnp.int32)
    tail_offsets = jnp.arange(WIN, dtype=jnp.int32)
    proj_own = jnp.einsum("kgd,grdf->grkf", own_keys, weight4, preferred_element_type=jnp.float32)
    first_set = (query4[:half_rows], query_pos[:half_rows])
    partner_start = (ctx_count - 1 - ctx_place) * local_rows
    visiting = visit_partner(query4[half_rows:])
    second_set = (visiting, partner_start + half_rows + jnp.arange(half_rows, dtype=jnp.int32))
    row_sets = (first_set, second_set)

    def add_tail(tails, key_block, value_block, key_pos):
        pick = (key_pos[None, :] == own_start - WIN + tail_offsets[:, None]).astype(jnp.bfloat16)
        return (
            tails[0]
            + jnp.einsum("wk,kgd->wgd", pick, key_block, preferred_element_type=jnp.float32),
            tails[1]
            + jnp.einsum("wk,kgd->wgd", pick, value_block, preferred_element_type=jnp.float32),
        )

    part_zero = (
        jnp.full((groups, group_ratio, half_rows), big_negative, jnp.float32),
        jnp.zeros((groups, group_ratio, half_rows), jnp.float32),
        jnp.zeros((groups, group_ratio, half_rows, HEAD_SIZE), jnp.float32),
    )
    tail_zero = (
        jnp.zeros((WIN, groups, HEAD_SIZE), jnp.float32),
        jnp.zeros((WIN, groups, HEAD_SIZE), jnp.float32),
    )
    state_zero = (
        jnp.zeros((groups, group_ratio, 2 * FM, HEAD_SIZE), jnp.float32),
        jnp.zeros((groups, group_ratio, 2 * FM), jnp.float32),
    )
    carry = ((part_zero, part_zero), tail_zero, ())
    key_piece = lax.all_gather(keys, "ctx", axis=0, tiled=True)
    value_piece = lax.all_gather(values, "ctx", axis=0, tiled=True)
    piece_rows = key_piece.shape[0]
    stride = math.gcd(piece_rows, local_rows)
    count = piece_rows // stride
    key_blocks = key_piece.reshape(count, stride, groups, HEAD_SIZE)
    value_blocks = value_piece.reshape(count, stride, groups, HEAD_SIZE)

    def fold_step(state, inputs):
        key_block, value_block, number = inputs
        first = number * stride
        key_pos = first + jnp.arange(stride, dtype=jnp.int32)
        parts_now, tails_now, states_now = state
        new_parts = (
            advance(parts_now[0], row_sets[0], key_block, value_block, key_pos, first),
            advance(parts_now[1], row_sets[1], key_block, value_block, key_pos, first),
        )
        earlier_block = first < own_start
        new_tails = lax.cond(
            earlier_block,
            lambda current: add_tail(current, key_block, value_block, key_pos),
            lambda current: current,
            tails_now,
        )
        return ((new_parts, new_tails, states_now), None)

    carry, unused = lax.scan(
        fold_step, carry, (key_blocks, value_blocks, jnp.arange(count, dtype=jnp.int32))
    )
    phi_own = features(proj_own)
    local_kv = split_product("grkf,kgd->grfd", phi_own, own_values)
    state_kv, state_norm = carried_in(
        (local_kv, jnp.sum(phi_own, axis=2)), "ctx", add_pair, state_zero
    )
    parts_done, tails_done = (carry[0], carry[1])
    teacher_first = parts_done[0][2] / parts_done[0][1][..., None]
    teacher_second = parts_done[1][2] / parts_done[1][1][..., None]
    teacher_second = return_partner(teacher_second)
    teacher = jnp.concatenate([teacher_first, teacher_second], axis=2)
    tail_key = tails_done[0].astype(jnp.bfloat16)
    tail_value = tails_done[1].astype(jnp.bfloat16)
    slab_key = jnp.concatenate([tail_key, own_keys], axis=0)
    slab_value = jnp.concatenate([tail_value, own_values], axis=0).astype(jnp.float32)
    slab_rows = WIN + local_rows
    slab_pos = own_start - WIN + jnp.arange(slab_rows, dtype=jnp.int32)
    is_tail = jnp.arange(slab_rows, dtype=jnp.int32) < WIN
    proj_tail = jnp.einsum("kgd,grdf->grkf", tail_key, weight4, preferred_element_type=jnp.float32)
    proj_slab = jnp.concatenate([proj_tail, proj_own], axis=2)
    phi_slab = features(proj_slab)
    proj_query = jnp.einsum("qgrd,grdf->grqf", query4, weight4, preferred_element_type=jnp.float32)
    phi_query = features(proj_query)
    scores = (
        jnp.einsum("qgrd,kgd->grqk", query4, slab_key, preferred_element_type=jnp.float32) * scale
    )
    window = (
        (slab_pos[None, :] >= query_pos[:, None] - WIN)
        & (slab_pos[None, :] <= query_pos[:, None])
        & (slab_pos[None, :] >= 0)
    )
    far = jnp.logical_not(is_tail)[None, :] & (slab_pos[None, :] < query_pos[:, None] - WIN)
    coefficient = far.astype(jnp.float32) - (window & is_tail[None, :]).astype(jnp.float32)
    window_top = jnp.max(jnp.where(window, scores, big_negative), axis=-1)
    local = jnp.exp(jnp.where(window, scores - window_top[..., None], big_negative))
    kernel = jnp.einsum("grqf,grkf->grqk", phi_query, phi_slab, precision=highest)
    mixed = local + coefficient * kernel
    numerator = jnp.einsum("grqk,kgd->grqd", mixed, slab_value, precision=highest) + jnp.einsum(
        "grqf,grfd->grqd", phi_query, state_kv, precision=highest
    )
    denominator = jnp.sum(mixed, axis=-1) + jnp.einsum(
        "grqf,grf->grq", phi_query, state_norm, precision=highest
    )
    student = numerator / denominator[..., None]
    error = student - teacher
    attn_error = jnp.transpose(error, (2, 0, 1, 3)).reshape(local_rows, heads_here * HEAD_SIZE)
    whole_rows = local_rows * ctx_count
    loss = lax.psum(jnp.sum(error * error), ("ctx", "head")) / (whole_rows * QUERY_HEADS)
    grad_out = 2.0 * error / denominator[..., None]
    grad_den = -jnp.sum(grad_out * student, axis=-1)
    later_kv = jnp.einsum("grqf,grqd->grfd", phi_query, grad_out, precision=highest)
    later_norm = jnp.einsum("grqf,grq->grf", phi_query, grad_den, precision=highest)
    suffix_kv, suffix_norm = prefix((later_kv, later_norm), "ctx", add_pair, state_zero)
    grad_lin = coefficient * (
        jnp.einsum("grqd,kgd->grqk", grad_out, slab_value, precision=highest) + grad_den[..., None]
    )
    grad_phi_query = (
        jnp.einsum("grqk,grkf->grqf", grad_lin, phi_slab, precision=highest)
        + jnp.einsum("grqd,grfd->grqf", grad_out, state_kv, precision=highest)
        + grad_den[..., None] * state_norm[:, :, None, :]
    )
    grad_phi_slab = jnp.einsum("grqk,grqf->grkf", grad_lin, phi_query, precision=highest)
    own_extra = (
        jnp.einsum("kgd,grfd->grkf", own_values.astype(jnp.float32), suffix_kv, precision=highest)
        + suffix_norm[:, :, None, :]
    )
    grad_phi_slab = grad_phi_slab + jnp.concatenate(
        [jnp.zeros((groups, group_ratio, WIN, 2 * FM), jnp.float32), own_extra], axis=2
    )
    grad_proj_query = feature_back(proj_query, grad_phi_query)
    grad_proj_slab = feature_back(proj_slab, grad_phi_slab)
    grad_local = jnp.einsum(
        "qgrd,grqf->grdf", query4.astype(jnp.float32), grad_proj_query, precision=highest
    ) + jnp.einsum(
        "kgd,grkf->grdf", slab_key.astype(jnp.float32), grad_proj_slab, precision=highest
    )
    grad_w = lax.psum(grad_local.reshape(heads_here, HEAD_SIZE, FM), "ctx")
    return (attn_error, loss, grad_w)


def solution(mesh):
    placed = (P("ctx", "head"), P("ctx", "head"), P("ctx", "head"), P("head", None, None))
    return jax.shard_map(
        shards,
        mesh=mesh,
        in_specs=placed,
        out_specs=(P("ctx", "head"), P(), P("head", None, None)),
        check_vma=False,
    )
```

profile of v0, /device:TPU:0, one launch (start us, length us, event | category | flops | bytes accessed | tf_op | source)
XLA Modules:
  0.0 783.3 jit_solution(9861084651910707477)
XLA Ops:
  29.9 8.6 %collective-permute-done.1 = bf16[64,4,8,128]{3,2,1,0:T(8,128)(2,1)} collective-permute-done((bf16[64,4,8,128]{3,2,1,0:T(8,128)(2,1)}, bf16[64,4,8,128]{3,2,1,0:T(8,128)(2,1)}, u32[]{:S(2)}, u32[]{:S(2)}) %collective-permute-start.1) | collective-permute-done | bytes 524320 | tf_op jit(solution)/shard_map/ppermute | solution.py:20
  40.3 5.5 fusion.79
  45.8 13.8 %collective-permute-done.2 = bf16[64,4,8,128]{3,2,1,0:T(8,128)(2,1)} collective-permute-done((bf16[64,4,8,128]{3,2,1,0:T(8,128)(2,1)}, bf16[64,4,8,128]{3,2,1,0:T(8,128)(2,1)}, u32[]{:S(2)}, u32[]{:S(2)}) %collective-permute-start.2) | collective-permute-done | bytes 524320 | tf_op jit(solution)/shard_map/ppermute | solution.py:20
  68.9 20.4 %collective-permute-done.3 = bf16[64,4,8,128]{3,2,1,0:T(8,128)(2,1)} collective-permute-done((bf16[64,4,8,128]{3,2,1,0:T(8,128)(2,1)}, bf16[64,4,8,128]{3,2,1,0:T(8,128)(2,1)}, u32[]{:S(2)}, u32[]{:S(2)}) %collective-permute-start.3) | collective-permute-done | bytes 524320 | tf_op jit(solution)/shard_map/ppermute | solution.py:20
  95.8 16.4 %all-gather.11.cloned.1.call-done = bf16[2048,512]{1,0:T(8,128)(2,1)} async-done(((bf16[128,512]{1,0:T(8,128)(2,1)}), bf16[2048,512]{1,0:T(8,128)(2,1)}) %all-gather.11.cloned.1.call-update) | async-done | bytes 2097168 | tf_op jit(solution)/shard_map/all_gather | solution.py:198
  118.3 193.6 %while.59 = (s32[]{:T(128)}, f32[4,8,64]{2,1,0:T(8,128)S(1)}, f32[4,8,64]{2,1,0:T(8,128)S(1)}, f32[4,8,64,128]{3,2,1,0:T(8,128)S(1)}, f32[4,8,64]{2,1,0:T(8,128)...) while((s32[]{:T(128)}, f32[4,8,64]{2,1,0:T(8,128)S(1)}, ...), condition=%wide.region_17.18_spmd.clone, body=%wide.region_0.17_spmd.clone.sunk | while | flops 291086528 | bytes 14226523 | solution.py:223
  316.5 64.0 %all-gather.1 = bf16[64,8,128]{2,1,0:T(8,128)(2,1)} all-gather(bf16[4,8,128]{2,1,0:T(8,128)(2,1)S(1)} %fusion.143), channel_id=3, replica_groups=mesh['ctx'=16,'head'=2] {'ctx'}, dimensions={0}, use_global_device_ids=true | all-gather | bytes 139264 | tf_op jit(solution)/shard_map/all_gather | solution.py:26
  389.1 4.7 fusion.109
  393.8 4.8 collective-permute-done.5
  400.9 11.1 %collective-permute-done.6 = bf16[4,8,64,128]{3,2,1,0:T(8,128)(2,1)S(1)} collective-permute-done((bf16[4,8,64,128]{3,2,1,0:T(8,128)(2,1)S(1)}, bf16[4,8,64,128]{3,2,1,0:T(8,128)(2,1)S(1)}, u32[]{:S(2)}, u32[]{:S(2)}) %collective-permute-start.6) | collective-permute-done | bytes 524320 | tf_op jit(solution)/shard_map/ppermute | solution.py:20
  413.3 5.2 fusion.122
  418.5 18.1 %collective-permute-done.7 = bf16[4,8,64,128]{3,2,1,0:T(8,128)(2,1)S(1)} collective-permute-done((bf16[4,8,64,128]{3,2,1,0:T(8,128)(2,1)S(1)}, bf16[4,8,64,128]{3,2,1,0:T(8,128)(2,1)S(1)}, u32[]{:S(2)}, u32[]{:S(2)}) %collective-permute-start.7) | collective-permute-done | bytes 524320 | tf_op jit(solution)/shard_map/ppermute | solution.py:20
  437.7 49.1 %while.60 = (s32[]{:T(128)}, f32[4,8,128,128]{3,2,1,0:T(8,128)S(1)}, f32[4,8,128]{2,1,0:T(8,128)S(1)}, s32[]{:T(128)}, bf16[16,4,8,128,128]{4,3,2,1,0:T(8,128)(2...) while((s32[]{:T(128)}, f32[4,8,128,128]{3,2,1,0:T(8,128)S(1)}, ...), condition=%wide.region_21.22_spmd.clone, body=%wide.region_20.21_spmd.clone.sunk | while | flops 2113540 | bytes 5283955 | solution.py:43
  486.7 5.7 fusion.150
  492.5 6.4 multiply_reduce_fusion
  509.0 19.1 %all-gather.3 = bf16[64,8,128]{2,1,0:T(8,128)(2,1)S(1)} all-gather(bf16[4,8,128]{2,1,0:T(8,128)(2,1)S(1)} %convert_element_type.142), channel_id=5, replica_groups=mesh['ctx'=16,'head'=2] {'ctx'}, dimensions={0}, use_global_device_ids=true | all-gather | bytes 139264 | tf_op jit(solution)/shard_map/all_gather | solution.py:49
  531.3 7.9 %fusion.68 = f32[4,8,128,128]{3,2,1,0:T(8,128)S(1)} fusion(f32[4,8,128,192]{2,3,1,0:T(8,128)S(1)} %fusion.121, f32[4,8,128]{2,1,0:T(8,128)S(1)} %neg.21, f32[128,192]{0,1:T(8,128)S(1)} %convert_subtract_fusion, f32[4,8,192,64]{3,2,1,0:T(8,128)S(1)} %copy-done.11, f32[4,8,192,64]{3,2,1,0:T(8,128)S(1)} %copy-done.9), kind=kOutput, calls=%fused_computation.116 | convolution fusion | flops 1211105280 | bytes 8503296 | tf_op jit(solution)/shard_map/grqk,grkf->grqf/dot_general | solution.py:282
  539.2 4.8 multiply_add_fusion.4
  548.6 81.4 %all-gather.15.cloned.1.call-done = bf16[64,8,128,128]{3,2,1,0:T(8,128)(2,1)} async-done(((bf16[4,8,128,128]{3,2,1,0:T(8,128)(2,1)}), bf16[64,8,128,128]{3,2,1,0:T(8,128)(2,1)}) %all-gather.15.cloned.1.call-update) | async-done | bytes 16777232 | tf_op jit(solution)/shard_map/all_gather | solution.py:49
  630.0 38.6 %while.61 = (s32[]{:T(128)}, f32[4,8,128,128]{3,2,1,0:T(8,128)S(1)}, f32[4,8,128]{2,1,0:T(8,128)S(1)}, s32[]{:T(128)}, bf16[16,4,8,128,128]{4,3,2,1,0:T(8,128)(2...) while((s32[]{:T(128)}, ...), condition=%wide.region_27.28_spmd.clone, body=%wide.region_26.27_spmd.clone.sunk | while | flops 2113544 | bytes 5284017 | solution.py:67
  670.2 5.7 pad_add_fusion
  675.9 5.3 fusion.102
  681.2 39.0 %psum.14 = f32[]{:T(128)} all-reduce(f32[]{:T(128)} %get-tuple-element.673), channel_id=1, replica_groups=mesh['ctx'=16,'head'=2] {'ctx','head'}, use_global_device_ids=true, to_apply=%region_24.25 | all-reduce | flops 1 | bytes 8 | tf_op jit(solution)/shard_map/psum | solution.py:272
  724.6 48.3 %all-reduce.3.cloned.1.call-done = f32[32,128,64]{1,2,0:T(8,128)} async-done(((f32[32,128,64]{1,2,0:T(8,128)}), f32[32,128,64]{1,2,0:T(8,128)}) %all-reduce.3.cloned.1.call-update) | async-done | bytes 1048592 | tf_op jit(solution)/shard_map/psum | solution.py:301
  (491 shorter events, 355.4 us)
Async XLA Ops:
  7.2 84.2 %all-gather.9.cloned.1.call-start = ((), (), s32[]{:S(2)}) async-start(), calls=%async_computation | async-start | bytes 2228224 | tf_op jit(solution)/shard_map/all_gather | solution.py:197
  7.9 104.2 %all-gather.11.cloned.1.call-start = ((), (), s32[]{:S(2)}) async-start(), calls=%async_computation.1 | async-start | bytes 2228224 | tf_op jit(solution)/shard_map/all_gather | solution.py:198
  8.7 429.0 %all-gather.13.cloned.1.call-start = ((), (), s32[]{:S(2)}) async-start(), calls=%async_computation.3 | async-start | bytes 17825792 | tf_op jit(solution)/shard_map/all_gather | solution.py:26
  10.8 53.0 %copy-start.22 = (bf16[128,512]{0,1:T(8,128)(2,1)}, bf16[128,512]{0,1:T(8,128)(2,1)S(1)}, u32[]{:S(2)}) copy-start(bf16[128,512]{0,1:T(8,128)(2,1)S(1)} %copy.138) | copy-start | bytes 393220
  17.9 612.1 %all-gather.15.cloned.1.call-start = ((), (), s32[]{:S(2)}) async-start(), calls=%async_computation.4 | async-start | bytes 17825792 | tf_op jit(solution)/shard_map/all_gather | solution.py:49
  20.1 2.9 collective-permute-start
  23.1 15.4 %collective-permute-start.1 = (bf16[64,4,8,128]{3,2,1,0:T(8,128)(2,1)}, bf16[64,4,8,128]{3,2,1,0:T(8,128)(2,1)}, u32[]{:S(2)}, u32[]{:S(2)}) collective-permute-start(bf16[64,4,8,128]{3,2,1,0:T(8,128)(2,1)} %collective-permute-done), channel_id=1, source_target_pairs={{0,4},{2,6},{4,0},{6,2},{8,12},{10,14},{12,8},{14,10},{16,20},{18,... | collective-permute-start | bytes 1572872 | tf_op jit(solution)/shard_map/ppermute | solution.py:20
  29.9 16.0 %copy-start.28 = (u8[4,128,64]{2,1,0:T(8,128)(4,1)}, u8[4,128,64]{2,1,0:T(8,128)(4,1)S(1)}, u32[]{:S(2)}) copy-start(u8[4,128,64]{2,1,0:T(8,128)(4,1)S(1)} %get-tuple-element.671) | copy-start | bytes 98308
  38.5 21.1 %collective-permute-start.2 = (bf16[64,4,8,128]{3,2,1,0:T(8,128)(2,1)}, bf16[64,4,8,128]{3,2,1,0:T(8,128)(2,1)}, u32[]{:S(2)}, u32[]{:S(2)}) collective-permute-start(bf16[64,4,8,128]{3,2,1,0:T(8,128)(2,1)} %collective-permute-done.1), channel_id=1, source_target_pairs={{0,8},{2,10},{4,12},{6,14},{8,0},{10,2},{12,4},{14,6},{16,24},{18,... | collective-permute-start | bytes 1572872 | tf_op jit(solution)/shard_map/ppermute | solution.py:20
  40.3 21.7 %copy-start.14 = (f32[4,8,128,64]{3,2,1,0:T(8,128)S(1)}, f32[4,8,128,64]{3,2,1,0:T(8,128)}, u32[]{:S(2)}) copy-start(f32[4,8,128,64]{3,2,1,0:T(8,128)} %copy-done.13) | copy-start | bytes 3145732
  59.6 29.8 %collective-permute-start.3 = (bf16[64,4,8,128]{3,2,1,0:T(8,128)(2,1)}, bf16[64,4,8,128]{3,2,1,0:T(8,128)(2,1)}, u32[]{:S(2)}, u32[]{:S(2)}) collective-permute-start(bf16[64,4,8,128]{3,2,1,0:T(8,128)(2,1)} %collective-permute-done.2), channel_id=1, source_target_pairs={{0,16},{2,18},{4,20},{6,22},{8,24},{10,26},{12,28},{14,30},{16,0},... | collective-permute-start | bytes 1572872 | tf_op jit(solution)/shard_map/ppermute | solution.py:20
  313.0 71.4 %collective-permute-start.4 = (bf16[4,8,64,128]{3,2,1,0:T(8,128)(2,1)}, bf16[4,8,64,128]{3,2,1,0:T(8,128)(2,1)S(1)}, u32[]{:S(2)}, u32[]{:S(2)}) collective-permute-start(bf16[4,8,64,128]{3,2,1,0:T(8,128)(2,1)} %divide_convert_fusion), channel_id=1, source_target_pairs={{0,2},{2,0},{4,6},{6,4},{8,10},{10,8},{12,14},{14,12},{16,18},{18,... | collective-permute-start | bytes 1572872 | tf_op jit(solution)/shard_map/ppermute | solution.py:20
  384.4 14.2 %collective-permute-start.5 = (bf16[4,8,64,128]{3,2,1,0:T(8,128)(2,1)S(1)}, bf16[4,8,64,128]{3,2,1,0:T(8,128)(2,1)S(1)}, u32[]{:S(2)}, u32[]{:S(2)}) collective-permute-start(bf16[4,8,64,128]{3,2,1,0:T(8,128)(2,1)S(1)} %collective-permute-done.4), channel_id=1, source_target_pairs={{0,4},{2,6},{4,0},{6,2},{8,12},{10,14},{12,8},{14,10},{16,20},{18,... | collective-permute-start | bytes 1572872 | tf_op jit(solution)/shard_map/ppermute | solution.py:20
  389.1 9.6 %copy-start.20 = (bf16[16,8,32,128]{3,2,1,0:T(8,128)(2,1)S(1)}, bf16[16,8,32,128]{3,2,1,0:T(8,128)(2,1)}, u32[]{:S(2)}) copy-start(bf16[16,8,32,128]{3,2,1,0:T(8,128)(2,1)} %copy.204) | copy-start | bytes 3145732
  389.1 9.6 %copy-start.27 = (bf16[128,4,128]{2,0,1:T(8,128)(2,1)S(1)}, bf16[128,4,128]{2,0,1:T(8,128)(2,1)}, u32[]{:S(2)}) copy-start(bf16[128,4,128]{2,0,1:T(8,128)(2,1)} %copy.128) | copy-start | bytes 393220
  398.6 13.4 %collective-permute-start.6 = (bf16[4,8,64,128]{3,2,1,0:T(8,128)(2,1)S(1)}, bf16[4,8,64,128]{3,2,1,0:T(8,128)(2,1)S(1)}, u32[]{:S(2)}, u32[]{:S(2)}) collective-permute-start(bf16[4,8,64,128]{3,2,1,0:T(8,128)(2,1)S(1)} %collective-permute-done.5), channel_id=1, source_target_pairs={{0,8},{2,10},{4,12},{6,14},{8,0},{10,2},{12,4},{14,6},{16,24},{18,... | collective-permute-start | bytes 1572872 | tf_op jit(solution)/shard_map/ppermute | solution.py:20
  400.9 12.4 %copy-start.26 = (bf16[128,4,128]{2,0,1:T(8,128)(2,1)S(1)}, bf16[128,4,128]{2,0,1:T(8,128)(2,1)}, u32[]{:S(2)}) copy-start(bf16[128,4,128]{2,0,1:T(8,128)(2,1)} %copy.139) | copy-start | bytes 393220
  412.0 24.6 %collective-permute-start.7 = (bf16[4,8,64,128]{3,2,1,0:T(8,128)(2,1)S(1)}, bf16[4,8,64,128]{3,2,1,0:T(8,128)(2,1)S(1)}, u32[]{:S(2)}, u32[]{:S(2)}) collective-permute-start(bf16[4,8,64,128]{3,2,1,0:T(8,128)(2,1)S(1)} %collective-permute-done.6), channel_id=1, source_target_pairs={{0,16},{2,18},{4,20},{6,22},{8,24},{10,26},{12,28},{14,30},{16,0},... | collective-permute-start | bytes 1572872 | tf_op jit(solution)/shard_map/ppermute | solution.py:20
  413.3 24.3 %copy-start.2 = (f32[4,8,128,128]{3,2,1,0:T(8,128)S(1)}, f32[4,8,128,128]{3,2,1,0:T(8,128)}, u32[]{:S(2)}) copy-start(f32[4,8,128,128]{3,2,1,0:T(8,128)} %custom-call) | copy-start | bytes 6291460
  486.7 12.1 %copy-start.3 = (f32[4,8,128,128]{3,2,1,0:T(8,128)}, f32[4,8,128,128]{3,2,1,0:T(8,128)S(1)}, u32[]{:S(2)}) copy-start(f32[4,8,128,128]{3,2,1,0:T(8,128)S(1)} %get-tuple-element.496) | copy-start | bytes 6291460
  504.8 268.1 %all-reduce.3.cloned.1.call-start = ((), (), s32[]{:S(2)}) async-start(), calls=%async_computation.2 | async-start | bytes 2097152 | tf_op jit(solution)/shard_map/psum | solution.py:301
  505.3 25.9 %copy-start.11 = (f32[4,8,192,64]{3,2,1,0:T(8,128)S(1)}, f32[4,8,192,64]{3,2,1,0:T(8,128)}, u32[]{:S(2)}) copy-start(f32[4,8,192,64]{3,2,1,0:T(8,128)} %copy-done.10) | copy-start | bytes 4718596
  630.0 38.6 %copy-start.23 = (bf16[128,512]{0,1:T(8,128)(2,1)S(1)}, bf16[128,512]{0,1:T(8,128)(2,1)}, u32[]{:S(2)}) copy-start(bf16[128,512]{0,1:T(8,128)(2,1)} %copy-done.22) | copy-start | bytes 393220
  722.1 53.1 %copy-start.1 = (bf16[32,128,64]{1,2,0:T(8,128)(2,1)S(1)}, bf16[32,128,64]{1,2,0:T(8,128)(2,1)}, u32[]{:S(2)}) copy-start(bf16[32,128,64]{1,2,0:T(8,128)(2,1)} %param.21) | copy-start | bytes 1572868
  (21 other events, 101.3 us)
Sparse Core Ops, SparseCore 0:
  10.2 45.6 all-gather.8
  58.0 54.1 all-gather.10
  114.3 125.7 all-gather.12
  505.0 124.9 all-gather.14
  681.3 91.5 all-reduce.2
where the time goes:
time: 796 us; the launch traced here: 783 us
  waiting for transfers between devices  224 us (28%)
  blocking collectives  122 us (15%)
  matrix products  120 us (15%)
  other arithmetic  120 us (15%)
  local copies, waits for them, and re-layouts  96.2 us (12%)
  loops' own time  72.7 us (9%)
  between operations  16.5 us (2%)
  starting transfers between devices  11 us (1%)
    all_gather x1, waiting for transfers between devices, prefix(): lax.all_gather(part.astype(kind), axis)  81.4 us
    ppermute x8, waiting for transfers between devices, swapped(): return lax.ppermute(value, axis, pairs)  76.8 us
    another operation x1, loops' own time, shards(): lax.scan(fold_step, carry, (key_blocks, value_blocks, jnp.arange(count, d...  70.5 us
    all_gather x1, blocking collectives, carried_in(): lax.all_gather(part.astype(kind), axis)  64 us
    select_n x32, other arithmetic, carried_step(): return jax.tree.map(lambda a, b: jnp.where(reached, a, b), new, before)  49 us
    psum x1, waiting for transfers between devices, shards(): grad_w = lax.psum(grad_local.reshape(heads_here, HEAD_SIZE, FM), 'ctx')  48.3 us
    psum x1, blocking collectives, shards(): lax.psum(jnp.sum(error * error), ('ctx', 'head'))  39 us
    dynamic_slice x64, local copies, waits for them, and re-layouts, shards(): lax.scan(fold_step, carry, (key_blocks, value_blocks, jnp.arange(count, d...  38.7 us
  transfers between devices with their start and end apart: 13, of which 9 were waited for; matrix products, arithmetic and copies ran while one was open for 28% of the time, Pallas kernels for 0%

commit v1 on v0

--- a/solution.py
+++ b/solution.py
@@ -195,7 +195,15 @@
     )
     carry = ((part_zero, part_zero), tail_zero, ())
     key_piece = lax.all_gather(keys, "ctx", axis=0, tiled=True)
-    value_piece = lax.all_gather(values, "ctx", axis=0, tiled=True)
+    ways, here_2 = (lax.axis_size("ctx"), lax.axis_index("ctx"))
+    grown, reach = (values, 1)
+    while reach < ways:
+        theirs = lax.ppermute(grown, "ctx", [(d, d ^ reach) for d in range(ways)])
+        mine_first = jnp.concatenate([grown, theirs], axis=0)
+        theirs_first = jnp.concatenate([theirs, grown], axis=0)
+        grown = jnp.where(here_2 & reach == 0, mine_first, theirs_first)
+        reach = 2 * reach
+    value_piece = grown
     piece_rows = key_piece.shape[0]
     stride = math.gcd(piece_rows, local_rows)
     count = piece_rows // stride

time: 796 us -> 840 us (1.055)
  waiting for transfers between devices: 224 us -> 263 us
    ppermute x0 -> x4, waiting for transfers between devices: none -> 57.4 us  [shards(): theirs = lax.ppermute(grown, 'ctx', [(d, d ^ reach) for d in range(ways)])]
    all_gather x1 -> x0, waiting for transfers between devices: 16.4 us -> none  [shards(): value_piece = lax.all_gather(values, 'ctx', axis=0, tiled=True)]
    ppermute x0 -> x4, starting transfers between devices: none -> 8.61 us  [shards(): theirs = lax.ppermute(grown, 'ctx', [(d, d ^ reach) for d in range(ways)])]
  transfers between devices with their start and end apart: 13 -> 16, of which waited for: 9 -> 12; matrix products, arithmetic and copies ran while one was open for 28% -> 26% of each run, Pallas kernels for 0% -> 0%
where the time goes in v1:
time: 840 us; the launch traced here: 831 us
  waiting for transfers between devices  263 us (31%)
  other arithmetic  124 us (15%)
  blocking collectives  122 us (15%)
  matrix products  119 us (14%)
  local copies, waits for them, and re-layouts  96.8 us (12%)
  loops' own time  71.7 us (9%)
  starting transfers between devices  17.9 us (2%)
  between operations  16.4 us (2%)
    all_gather x1, waiting for transfers between devices, prefix(): lax.all_gather(part.astype(kind), axis)  81.1 us
    ppermute x8, waiting for transfers between devices, swapped(): return lax.ppermute(value, axis, pairs)  75.5 us
    another operation x1, loops' own time, shards(): lax.scan(fold_step, carry, (key_blocks, value_blocks, jnp.arange(count, d...  69.6 us
    all_gather x1, blocking collectives, carried_in(): lax.all_gather(part.astype(kind), axis)  63.9 us
    ppermute x4, waiting for transfers between devices, shards(): theirs = lax.ppermute(grown, 'ctx', [(d, d ^ reach) for d in range(ways)])  57.4 us
    select_n x32, other arithmetic, carried_step(): return jax.tree.map(lambda a, b: jnp.where(reached, a, b), new, before)  49 us
    psum x1, waiting for transfers between devices, shards(): grad_w = lax.psum(grad_local.reshape(heads_here, HEAD_SIZE, FM), 'ctx')  48.3 us
    psum x1, blocking collectives, shards(): lax.psum(jnp.sum(error * error), ('ctx', 'head'))  38.9 us
  transfers between devices with their start and end apart: 16, of which 12 were waited for; matrix products, arithmetic and copies ran while one was open for 26% of the time, Pallas kernels for 0%

profile of v1, /device:TPU:0, one launch (start us, length us, event | category | flops | bytes accessed | tf_op | source)
XLA Modules:
  0.0 831.1 jit_solution(527087233811665068)
XLA Ops:
  37.6 12.2 %collective-permute-done.2 = bf16[512,512]{1,0:T(8,128)(2,1)} collective-permute-done((bf16[512,512]{1,0:T(8,128)(2,1)S(1)}, bf16[512,512]{1,0:T(8,128)(2,1)}, u32[]{:S(2)}, u32[]{:S(2)}) %collective-permute-start.2) | collective-permute-done | bytes 524320 | tf_op jit(solution)/shard_map/ppermute | solution.py:201
  61.1 28.5 %collective-permute-done.6 = bf16[64,4,8,128]{3,2,1,0:T(8,128)(2,1)} collective-permute-done((bf16[64,4,8,128]{3,2,1,0:T(8,128)(2,1)}, bf16[64,4,8,128]{3,2,1,0:T(8,128)(2,1)}, u32[]{:S(2)}, u32[]{:S(2)}) %collective-permute-start.6) | collective-permute-done | bytes 524320 | tf_op jit(solution)/shard_map/ppermute | solution.py:20
  97.3 40.5 %collective-permute-done.3 = bf16[1024,512]{1,0:T(8,128)(2,1)} collective-permute-done((bf16[1024,512]{1,0:T(8,128)(2,1)}, bf16[1024,512]{1,0:T(8,128)(2,1)}, u32[]{:S(2)}, u32[]{:S(2)}) %collective-permute-start.3) | collective-permute-done | bytes 1048608 | tf_op jit(solution)/shard_map/ppermute | solution.py:201
  146.6 12.9 %collective-permute-done.7 = bf16[64,4,8,128]{3,2,1,0:T(8,128)(2,1)} collective-permute-done((bf16[64,4,8,128]{3,2,1,0:T(8,128)(2,1)}, bf16[64,4,8,128]{3,2,1,0:T(8,128)(2,1)}, u32[]{:S(2)}, u32[]{:S(2)}) %collective-permute-start.7) | collective-permute-done | bytes 524320 | tf_op jit(solution)/shard_map/ppermute | solution.py:20
  167.9 192.6 %while.59 = (s32[]{:T(128)}, f32[4,8,64]{2,1,0:T(8,128)S(1)}, f32[4,8,64]{2,1,0:T(8,128)S(1)}, f32[4,8,64,128]{3,2,1,0:T(8,128)S(1)}, f32[4,8,64]{2,1,0:T(8,128)...) while((s32[]{:T(128)}, f32[4,8,64]{2,1,0:T(8,128)S(1)}, ...), condition=%wide.region_17.18_spmd.clone, body=%wide.region_0.17_spmd.clone.sunk | while | flops 291086528 | bytes 14226523 | solution.py:231
  364.0 63.9 %all-gather.1 = bf16[64,8,128]{2,1,0:T(8,128)(2,1)} all-gather(bf16[4,8,128]{2,1,0:T(8,128)(2,1)S(1)} %fusion.143), channel_id=3, replica_groups=mesh['ctx'=16,'head'=2] {'ctx'}, dimensions={0}, use_global_device_ids=true | all-gather | bytes 139264 | tf_op jit(solution)/shard_map/all_gather | solution.py:26
  437.2 4.7 fusion.109
  441.9 4.8 collective-permute-done.9
  449.0 11.1 %collective-permute-done.10 = bf16[4,8,64,128]{3,2,1,0:T(8,128)(2,1)S(1)} collective-permute-done((bf16[4,8,64,128]{3,2,1,0:T(8,128)(2,1)S(1)}, bf16[4,8,64,128]{3,2,1,0:T(8,128)(2,1)S(1)}, u32[]{:S(2)}, u32[]{:S(2)}) %collective-permute-start.10) | collective-permute-done | bytes 524320 | tf_op jit(solution)/shard_map/ppermute | solution.py:20
  461.4 5.2 fusion.122
  466.6 18.0 %collective-permute-done.11 = bf16[4,8,64,128]{3,2,1,0:T(8,128)(2,1)S(1)} collective-permute-done((bf16[4,8,64,128]{3,2,1,0:T(8,128)(2,1)S(1)}, bf16[4,8,64,128]{3,2,1,0:T(8,128)(2,1)S(1)}, u32[]{:S(2)}, u32[]{:S(2)}) %collective-permute-start.11) | collective-permute-done | bytes 524320 | tf_op jit(solution)/shard_map/ppermute | solution.py:20
  485.8 49.1 %while.60 = (s32[]{:T(128)}, f32[4,8,128,128]{3,2,1,0:T(8,128)S(1)}, f32[4,8,128]{2,1,0:T(8,128)S(1)}, s32[]{:T(128)}, bf16[16,4,8,128,128]{4,3,2,1,0:T(8,128)(2...) while((s32[]{:T(128)}, f32[4,8,128,128]{3,2,1,0:T(8,128)S(1)}, ...), condition=%wide.region_21.22_spmd.clone, body=%wide.region_20.21_spmd.clone.sunk | while | flops 2113540 | bytes 5283955 | solution.py:43
  534.8 5.7 fusion.150
  540.6 6.4 multiply_reduce_fusion
  548.3 4.6 convolution_convert_fusion
  557.1 19.3 %all-gather.3 = bf16[64,8,128]{2,1,0:T(8,128)(2,1)S(1)} all-gather(bf16[4,8,128]{2,1,0:T(8,128)(2,1)S(1)} %convert_element_type.142), channel_id=5, replica_groups=mesh['ctx'=16,'head'=2] {'ctx'}, dimensions={0}, use_global_device_ids=true | all-gather | bytes 139264 | tf_op jit(solution)/shard_map/all_gather | solution.py:49
  579.7 7.9 fusion.68
  587.6 4.8 multiply_add_fusion.4
  596.9 81.1 %all-gather.12.cloned.1.call-done = bf16[64,8,128,128]{3,2,1,0:T(8,128)(2,1)} async-done(((bf16[4,8,128,128]{3,2,1,0:T(8,128)(2,1)}), bf16[64,8,128,128]{3,2,1,0:T(8,128)(2,1)}) %all-gather.12.cloned.1.call-update) | async-done | bytes 16777232 | tf_op jit(solution)/shard_map/all_gather | solution.py:49
  678.0 38.6 %while.61 = (s32[]{:T(128)}, f32[4,8,128,128]{3,2,1,0:T(8,128)S(1)}, f32[4,8,128]{2,1,0:T(8,128)S(1)}, s32[]{:T(128)}, bf16[16,4,8,128,128]{4,3,2,1,0:T(8,128)(2...) while((s32[]{:T(128)}, ...), condition=%wide.region_27.28_spmd.clone, body=%wide.region_26.27_spmd.clone.sunk | while | flops 2113544 | bytes 5284017 | solution.py:67
  718.2 5.7 pad_add_fusion
  724.0 5.3 fusion.102
  729.3 38.9 %psum.14 = f32[]{:T(128)} all-reduce(f32[]{:T(128)} %get-tuple-element.673), channel_id=1, replica_groups=mesh['ctx'=16,'head'=2] {'ctx','head'}, use_global_device_ids=true, to_apply=%region_24.25 | all-reduce | flops 1 | bytes 8 | tf_op jit(solution)/shard_map/psum | solution.py:280
  772.6 48.3 %all-reduce.3.cloned.1.call-done = f32[32,128,64]{1,2,0:T(8,128)} async-done(((f32[32,128,64]{1,2,0:T(8,128)}), f32[32,128,64]{1,2,0:T(8,128)}) %all-reduce.3.cloned.1.call-update) | async-done | bytes 1048592 | tf_op jit(solution)/shard_map/psum | solution.py:309
  (512 shorter events, 370.3 us)
Async XLA Ops:
  7.2 154.4 %all-gather.8.cloned.1.call-start = ((), (), s32[]{:S(2)}) async-start(), calls=%async_computation | async-start | bytes 2228224 | tf_op jit(solution)/shard_map/all_gather | solution.py:197
  7.9 477.8 %all-gather.10.cloned.1.call-start = ((), (), s32[]{:S(2)}) async-start(), calls=%async_computation.2 | async-start | bytes 17825792 | tf_op jit(solution)/shard_map/all_gather | solution.py:26
  10.1 86.4 %copy-start.23 = (bf16[128,512]{0,1:T(8,128)(2,1)}, bf16[128,512]{0,1:T(8,128)(2,1)S(1)}, u32[]{:S(2)}) copy-start(bf16[128,512]{0,1:T(8,128)(2,1)S(1)} %copy.138) | copy-start | bytes 393220
  17.2 660.8 %all-gather.12.cloned.1.call-start = ((), (), s32[]{:S(2)}) async-start(), calls=%async_computation.3 | async-start | bytes 17825792 | tf_op jit(solution)/shard_map/all_gather | solution.py:49
  17.6 1.5 collective-permute-start
  19.2 11.1 %collective-permute-start.1 = (bf16[256,512]{1,0:T(8,128)(2,1)S(1)}, bf16[256,512]{1,0:T(8,128)(2,1)}, u32[]{:S(2)}, u32[]{:S(2)}) collective-permute-start(bf16[256,512]{1,0:T(8,128)(2,1)S(1)} %maximum_select_fusion.3), channel_id=1, source_target_pairs={{0,4},{2,6},{4,0},{6,2},{8,12},{10,14},{12,8},{14,10},{16,20},{18,... | collective-permute-start | bytes 786440 | tf_op jit(solution)/shard_map/ppermute | solution.py:201
  25.1 11.3 %collective-permute-start.4 = (bf16[64,4,8,128]{3,2,1,0:T(8,128)(2,1)}, bf16[64,4,8,128]{3,2,1,0:T(8,128)(2,1)}, u32[]{:S(2)}, u32[]{:S(2)}) collective-permute-start(bf16[64,4,8,128]{3,2,1,0:T(8,128)(2,1)} %bitcast.96), channel_id=1, source_target_pairs={{0,2},{2,0},{4,6},{6,4},{8,10},{10,8},{12,14},{14,12},{16,18},{18,... | collective-permute-start | bytes 1572872 | tf_op jit(solution)/shard_map/ppermute | solution.py:20
  31.4 18.4 %collective-permute-start.2 = (bf16[512,512]{1,0:T(8,128)(2,1)S(1)}, bf16[512,512]{1,0:T(8,128)(2,1)}, u32[]{:S(2)}, u32[]{:S(2)}) collective-permute-start(bf16[512,512]{1,0:T(8,128)(2,1)S(1)} %maximum_select_fusion.2), channel_id=1, source_target_pairs={{0,8},{2,10},{4,12},{6,14},{8,0},{10,2},{12,4},{14,6},{16,24},{18,... | collective-permute-start | bytes 1572872 | tf_op jit(solution)/shard_map/ppermute | solution.py:201
  36.4 22.7 %copy-start.34 = (u8[4,128,64]{2,1,0:T(8,128)(4,1)}, u8[4,128,64]{2,1,0:T(8,128)(4,1)S(1)}, u32[]{:S(2)}) copy-start(u8[4,128,64]{2,1,0:T(8,128)(4,1)S(1)} %get-tuple-element.671) | copy-start | bytes 98308
  36.4 19.5 %collective-permute-start.5 = (bf16[64,4,8,128]{3,2,1,0:T(8,128)(2,1)}, bf16[64,4,8,128]{3,2,1,0:T(8,128)(2,1)}, u32[]{:S(2)}, u32[]{:S(2)}) collective-permute-start(bf16[64,4,8,128]{3,2,1,0:T(8,128)(2,1)} %collective-permute-done.4), channel_id=1, source_target_pairs={{0,4},{2,6},{4,0},{6,2},{8,12},{10,14},{12,8},{14,10},{16,20},{18,... | collective-permute-start | bytes 1572872 | tf_op jit(solution)/shard_map/ppermute | solution.py:20
  52.4 85.4 %collective-permute-start.3 = (bf16[1024,512]{1,0:T(8,128)(2,1)}, bf16[1024,512]{1,0:T(8,128)(2,1)}, u32[]{:S(2)}, u32[]{:S(2)}) collective-permute-start(bf16[1024,512]{1,0:T(8,128)(2,1)} %maximum_select_fusion.1), channel_id=1, source_target_pairs={{0,16},{2,18},{4,20},{6,22},{8,24},{10,26},{12,28},{14,30},{16,0},... | collective-permute-start | bytes 3145736 | tf_op jit(solution)/shard_map/ppermute | solution.py:201
  55.9 33.7 %collective-permute-start.6 = (bf16[64,4,8,128]{3,2,1,0:T(8,128)(2,1)}, bf16[64,4,8,128]{3,2,1,0:T(8,128)(2,1)}, u32[]{:S(2)}, u32[]{:S(2)}) collective-permute-start(bf16[64,4,8,128]{3,2,1,0:T(8,128)(2,1)} %collective-permute-done.5), channel_id=1, source_target_pairs={{0,8},{2,10},{4,12},{6,14},{8,0},{10,2},{12,4},{14,6},{16,24},{18,... | collective-permute-start | bytes 1572872 | tf_op jit(solution)/shard_map/ppermute | solution.py:20
  59.1 34.9 %copy-start.14 = (f32[4,8,128,64]{3,2,1,0:T(8,128)S(1)}, f32[4,8,128,64]{3,2,1,0:T(8,128)}, u32[]{:S(2)}) copy-start(f32[4,8,128,64]{3,2,1,0:T(8,128)} %copy-done.13) | copy-start | bytes 3145732
  61.0 33.8 %copy-start.27 = (bf16[8,8,32,128]{3,1,2,0:T(8,128)(2,1)S(1)}, bf16[8,8,32,128]{3,1,2,0:T(8,128)(2,1)}, u32[]{:S(2)}) copy-start(bf16[8,8,32,128]{3,1,2,0:T(8,128)(2,1)} %get-tuple-element.765) | copy-start | bytes 1572868
  89.6 69.9 %collective-permute-start.7 = (bf16[64,4,8,128]{3,2,1,0:T(8,128)(2,1)}, bf16[64,4,8,128]{3,2,1,0:T(8,128)(2,1)}, u32[]{:S(2)}, u32[]{:S(2)}) collective-permute-start(bf16[64,4,8,128]{3,2,1,0:T(8,128)(2,1)} %collective-permute-done.6), channel_id=1, source_target_pairs={{0,16},{2,18},{4,20},{6,22},{8,24},{10,26},{12,28},{14,30},{16,0},... | collective-permute-start | bytes 1572872 | tf_op jit(solution)/shard_map/ppermute | solution.py:20
  361.6 70.9 %collective-permute-start.8 = (bf16[4,8,64,128]{3,2,1,0:T(8,128)(2,1)}, bf16[4,8,64,128]{3,2,1,0:T(8,128)(2,1)S(1)}, u32[]{:S(2)}, u32[]{:S(2)}) collective-permute-start(bf16[4,8,64,128]{3,2,1,0:T(8,128)(2,1)} %divide_convert_fusion), channel_id=1, source_target_pairs={{0,2},{2,0},{4,6},{6,4},{8,10},{10,8},{12,14},{14,12},{16,18},{18,... | collective-permute-start | bytes 1572872 | tf_op jit(solution)/shard_map/ppermute | solution.py:20
  432.5 14.2 %collective-permute-start.9 = (bf16[4,8,64,128]{3,2,1,0:T(8,128)(2,1)S(1)}, bf16[4,8,64,128]{3,2,1,0:T(8,128)(2,1)S(1)}, u32[]{:S(2)}, u32[]{:S(2)}) collective-permute-start(bf16[4,8,64,128]{3,2,1,0:T(8,128)(2,1)S(1)} %collective-permute-done.8), channel_id=1, source_target_pairs={{0,4},{2,6},{4,0},{6,2},{8,12},{10,14},{12,8},{14,10},{16,20},{18,... | collective-permute-start | bytes 1572872 | tf_op jit(solution)/shard_map/ppermute | solution.py:20
  446.7 13.4 %collective-permute-start.10 = (bf16[4,8,64,128]{3,2,1,0:T(8,128)(2,1)S(1)}, bf16[4,8,64,128]{3,2,1,0:T(8,128)(2,1)S(1)}, u32[]{:S(2)}, u32[]{:S(2)}) collective-permute-start(bf16[4,8,64,128]{3,2,1,0:T(8,128)(2,1)S(1)} %collective-permute-done.9), channel_id=1, source_target_pairs={{0,8},{2,10},{4,12},{6,14},{8,0},{10,2},{12,4},{14,6},{16,24},{18,... | collective-permute-start | bytes 1572872 | tf_op jit(solution)/shard_map/ppermute | solution.py:20
  460.1 24.6 %collective-permute-start.11 = (bf16[4,8,64,128]{3,2,1,0:T(8,128)(2,1)S(1)}, bf16[4,8,64,128]{3,2,1,0:T(8,128)(2,1)S(1)}, u32[]{:S(2)}, u32[]{:S(2)}) collective-permute-start(bf16[4,8,64,128]{3,2,1,0:T(8,128)(2,1)S(1)} %collective-permute-done.10), channel_id=1, source_target_pairs={{0,16},{2,18},{4,20},{6,22},{8,24},{10,26},{12,28},{14,30},{16,0},... | collective-permute-start | bytes 1572872 | tf_op jit(solution)/shard_map/ppermute | solution.py:20
  461.4 24.3 %copy-start.2 = (f32[4,8,128,128]{3,2,1,0:T(8,128)S(1)}, f32[4,8,128,128]{3,2,1,0:T(8,128)}, u32[]{:S(2)}) copy-start(f32[4,8,128,128]{3,2,1,0:T(8,128)} %custom-call) | copy-start | bytes 6291460
  552.9 267.9 %all-reduce.3.cloned.1.call-start = ((), (), s32[]{:S(2)}) async-start(), calls=%async_computation.1 | async-start | bytes 2097152 | tf_op jit(solution)/shard_map/psum | solution.py:309
  553.4 26.2 %copy-start.11 = (f32[4,8,192,64]{3,2,1,0:T(8,128)S(1)}, f32[4,8,192,64]{3,2,1,0:T(8,128)}, u32[]{:S(2)}) copy-start(f32[4,8,192,64]{3,2,1,0:T(8,128)} %copy-done.10) | copy-start | bytes 4718596
  678.0 38.6 %copy-start.24 = (bf16[128,512]{0,1:T(8,128)(2,1)S(1)}, bf16[128,512]{0,1:T(8,128)(2,1)}, u32[]{:S(2)}) copy-start(bf16[128,512]{0,1:T(8,128)(2,1)} %copy-done.23) | copy-start | bytes 393220
  770.1 53.1 %copy-start.1 = (bf16[32,128,64]{1,2,0:T(8,128)(2,1)S(1)}, bf16[32,128,64]{1,2,0:T(8,128)(2,1)}, u32[]{:S(2)}) copy-start(bf16[32,128,64]{1,2,0:T(8,128)(2,1)} %param.21) | copy-start | bytes 1572868
  (30 other events, 182.5 us)
Sparse Core Ops, SparseCore 0:
  10.2 73.5 all-gather.7
  85.9 151.4 all-gather.9
  553.1 124.8 all-gather.11
  729.4 91.4 all-reduce.2
